TPU v7x, 32 devices: a whole 2x2x4 slice. The times are simulated.
32 devices in a mesh: blk: 16 (over z, y, core), rep: 2 (over x).
Axes of the slice: x: 2, y: 2, z: 4, core: 2. Of those that a mesh axis runs over, the one named last changes fastest.
Arguments:
- features: bfloat16 [32768, 256], P(('blk', 'rep')), may hold values from -6 to 6
- aggregated: bfloat16 [32768, 256], P(('blk', 'rep')), may hold values from -6 to 6
- out_grad: bfloat16 [32768, 256], P(('blk', 'rep')), may hold values from -6 to 6
- w_self: bfloat16 [256, 256], replicated, may hold values from -0.375 to 0.375
- w_neigh: bfloat16 [256, 256], replicated, may hold values from -0.375 to 0.375
- tiles: bfloat16 [16, 16, 8, 128, 128], P('blk'), may hold values from -0.0625 to 0.0625
- tile_rows: int32 [16, 16, 8], P('blk'), may hold values from 0 to 15
- tile_cols: int32 [16, 16, 8], P('blk'), may hold values from 0 to 15
- tile_counts: int32 [16, 16], P('blk'), may hold values from 0 to 8, as said below
Outputs:
- feature_grad: float32 [32768, 256], P(('blk', 'rep'))
- self_grad: float32 [256, 256], replicated
- neigh_grad: float32 [256, 256], replicated
Inputs may be any that keep to these rules, and one draw needn't show every extreme that they name: `tile_counts`: at most 8; some pair of blocks uses all 8 slots; tiles, rows and columns of slots beyond the count carry no meaning.
All inputs are finite; a program needn't handle non-finite values.
Results may differ from a plain program's by a relative error of at most 0.00082.
Values may be sent and summed in bfloat16 or wider, within the bound.
A program may use at most 64 MiB of HBM per device.

v0:
```python
import jax
import jax.numpy as jnp
from jax import lax
from jax.sharding import PartitionSpec as P


def on_device(
    features, aggregated, out_grad, w_self, w_neigh, tiles, tile_rows, tile_cols, tile_counts
):
    block_total = lax.axis_size("blk")
    copies = lax.axis_size("rep")
    replica = lax.axis_index("rep")
    width = out_grad.shape[1]
    side = tiles.shape[-1]
    slots_total = tiles.shape[2]
    share = jnp.dot(out_grad, w_neigh.T, preferred_element_type=jnp.float32).astype(jnp.bfloat16)
    whole = lax.all_gather(share, "rep", axis=0, tiled=True)
    block_rows = whole.shape[0]
    tiles_side = block_rows // side
    pieces_whole = whole.reshape(tiles_side, side, width)
    per_copy = (slots_total + copies - 1) // copies
    slot_ids = replica + copies * jnp.arange(per_copy, dtype=jnp.int32)
    valid = slot_ids < slots_total
    safe = jnp.minimum(slot_ids, slots_total - 1)
    wanted = jnp.take(tile_cols[0], safe, axis=1)
    found = pieces_whole[lax.all_to_all(wanted, "blk", split_axis=0, concat_axis=0, tiled=True)]
    fetched = lax.all_to_all(found, "blk", split_axis=0, concat_axis=0, tiled=True)
    chosen_tiles = jnp.take(tiles[0], safe, axis=1)
    products = jnp.einsum(
        "ikpq,ikqf->ikpf", chosen_tiles, fetched, preferred_element_type=jnp.float32
    )
    live = valid[None, :] & (slot_ids[None, :] < tile_counts[0][:, None])
    products = jnp.where(live[:, :, None, None], products, jnp.zeros_like(products))
    target_rows = jnp.take(tile_rows[0], safe, axis=1).reshape(-1)
    accumulated = jnp.zeros((tiles_side, side, width), jnp.float32)
    accumulated = accumulated.at[target_rows].add(products.reshape(-1, side, width))
    flat = accumulated.reshape(block_rows, width)
    self_part = jnp.dot(out_grad, w_self.T, preferred_element_type=jnp.float32)
    contract = (((0,), (0,)), ((), ()))
    terms_self = lax.dot_general(features, out_grad, contract, preferred_element_type=jnp.float32)
    terms_neigh = lax.dot_general(
        aggregated, out_grad, contract, preferred_element_type=jnp.float32
    )
    scale = (out_grad.shape[0] * block_total * copies) ** (-0.5)
    spread_share = lax.psum_scatter(flat, "rep", scatter_dimension=0, tiled=True)
    self_sum, neigh_sum = lax.psum((terms_self, terms_neigh), ("blk", "rep"))
    return (spread_share + self_part, self_sum * scale, neigh_sum * scale)


def solution(mesh):
    placed = (
        P(("blk", "rep"), None),
        P(("blk", "rep"), None),
        P(("blk", "rep"), None),
        P(),
        P(),
        P("blk", None, None, None, None),
        P("blk", None, None),
        P("blk", None, None),
        P("blk", None),
    )
    return jax.shard_map(
        on_device,
        mesh=mesh,
        in_specs=placed,
        out_specs=(P(("blk", "rep"), None), P(), P()),
        check_vma=False,
    )
```

profile of v0, /device:TPU:0, one launch (start us, length us, event | category | flops | bytes accessed | tf_op | source)
XLA Modules:
  0.0 258.7 jit_solution(6246822400090032343)
XLA Ops:
  8.0 0.0 copy-start
  8.0 0.0 all-gather.2.cloned.1.call-start
  8.1 1.0 copy-done
  9.0 2.0 convolution_convert_fusion
  11.1 0.0 all-gather.2.cloned.1.call-update
  11.1 1.2 gather_fusion.2
  12.4 1.2 gather_fusion.3
  13.6 0.1 select_bitcast_fusion.1
  13.7 0.1 copy.25
  13.8 13.6 %all_to_all.17 = s32[16,1,4]{2,1,0:T(1,128)S(1)} all-to-all(s32[16,1,4]{2,1,0:T(1,128)S(1)} %copy.25), channel_id=1, replica_groups=mesh['blk'=16,'rep'=2] {'blk'}, dimensions={0} | all-to-all | bytes 512 | tf_op jit(solution)/shard_map/all_to_all | solution.py:26
  27.4 0.1 copy.26
  27.5 0.1 copy.27
  27.6 0.1 reshape.190
  27.7 7.5 %all-gather.2.cloned.1.call-done = bf16[2048,256]{1,0:T(8,128)(2,1)} async-done(((bf16[1024,256]{1,0:T(8,128)(2,1)}), bf16[2048,256]{1,0:T(8,128)(2,1)}) %all-gather.2.cloned.1.call-update) | async-done | bytes 1048592 | tf_op jit(solution)/shard_map/all_gather | solution.py:17
  35.2 4.0 %gather_fusion.1 = bf16[64,128,256]{2,1,0:T(8,128)(2,1)} fusion(bf16[16,128,256]{2,1,0:T(8,128)(2,1)} %bitcast.37, s32[1024]{0:T(1024)S(1)} %pad_clamp_fusion), kind=kCustom, calls=%fused_computation.3 | custom fusion | bytes 8388864 | tf_op jit(solution)/shard_map/gather | solution.py:26
  39.2 0.0 copy-start.2
  39.2 0.0 copy-start.3
  39.2 0.0 copy-start.5
  39.2 5.8 %all-to-all-start.1 = ((bf16[16,4,128,256]{3,2,1,0:T(8,128)(2,1)}), bf16[16,4,128,256]{3,2,1,0:T(8,128)(2,1)}, u32[]{:S(2)}, u32[]{:S(2)}) async-start(bf16[16,4,128,256]{3,2,1,0:T(8,128)(2,1)} %bitcast.38), calls=%async_computation.1 | async-start | bytes 8388608 | tf_op jit(solution)/shard_map/all_to_all | solution.py:27
  45.1 0.0 all-reduce.3.cloned.1.call-start
  45.1 0.0 copy-done.2
  45.1 1.0 fusion.3
  46.2 0.0 copy-done.3
  46.2 1.0 fusion.4
  47.2 0.0 all-reduce.3.cloned.1.call-update
  47.2 0.0 reduce-scatter.2.cloned.1.call-start
  47.3 0.0 copy-done.5
  47.3 0.1 compare_and_fusion.1
  47.4 0.1 copy.24
  47.5 0.1 copy.23
  47.5 0.1 reshape.160
  47.7 3.1 %gather_fusion = bf16[4,16,128,128]{3,2,1,0:T(8,128)(2,1)S(1)} fusion(bf16[16,8,128,128]{3,2,1,0:T(8,128)(2,1)} %bitcast.41, s32[1024]{0:T(1024)S(1)} %pad_clamp_fusion.1), kind=kCustom, calls=%fused_computation.2 | custom fusion | bytes 4194320 | tf_op jit(solution)/shard_map/jit(_take)/gather | solution.py:28
  50.8 74.2 %all-to-all-done.1 = bf16[16,4,128,256]{3,2,1,0:T(8,128)(2,1)} async-done(((bf16[16,4,128,256]{3,2,1,0:T(8,128)(2,1)}), bf16[16,4,128,256]{3,2,1,0:T(8,128)(2,1)}, u32[]{:S(2)}, u32[]{:S(2)}) %all-to-all-start.1) | async-done | bytes 4194336 | tf_op jit(solution)/shard_map/all_to_all | solution.py:27
  125.0 6.7 %broadcast_select_fusion = f32[16,4,128,256]{3,2,1,0:T(8,128)} fusion(pred[16,4]{1,0:T(8,128)(4,1)S(1)} %copy.24, bf16[16,4,128,256]{3,2,1,0:T(8,128)(2,1)} %all-to-all-done.1, bf16[4,16,128,128]{3,2,1,0:T(8,128)(2,1)S(1)} %gather_fusion, pred[4]{0:T(512)(128)(4,1)S(1)} %get-tuple-element.10), kind=kOutput, calls=%fused_computation.5 | convolution fusion | flops 540016640 | bytes 14680132 | tf_op jit(solution)/shard_map/ikpq,ikqf->ikpf/dot_general | solution.py:29
  131.8 0.2 broadcast_in_dim.38
  132.0 0.0 copy-start.4
  132.0 12.5 %scatter_fusion = f32[16,128,256]{2,1,0:T(8,128)S(1)} fusion(f32[16,128,256]{2,1,0:T(8,128)S(1)} %broadcast_in_dim.38, s32[64]{0:T(128)S(1)} %fusion.1, f32[64,128,256]{2,1,0:T(8,128)} %bitcast.36), kind=kCustom, calls=%fused_computation.4 | custom fusion | flops 2097152 | bytes 25166080 | tf_op jit(solution)/shard_map/scatter-add | solution.py:36
  144.5 0.0 copy-start.1
  144.5 1.3 copy-done.1
  145.8 0.0 reduce-scatter.2.cloned.1.call-update
  145.8 101.1 %all-reduce.3.cloned.1.call-done = (f32[256,256]{1,0:T(8,128)}, f32[256,256]{1,0:T(8,128)}) async-done(((f32[256,256]{1,0:T(8,128)}, f32[256,256]{1,0:T(8,128)}), (f32[256,256]{1,0:T(8,128)}, f32[256,256]{1,0:T(8,128)})) %all-reduce.3.cloned.1.call-update) | async-done | bytes 524304 | tf_op jit(solution)/shard_map/psum | solution.py:46
  246.9 1.9 broadcast_multiply_fusion
  248.8 0.0 reduce-scatter.2.cloned.1.call-done
  248.8 0.0 copy-done.4
  248.8 2.5 convolution_add_fusion
  (8 shorter events, 0.1 us)
Async XLA Ops:
  8.0 1.0 copy-start
  8.0 27.2 %all-gather.2.cloned.1.call-start = ((), (), s32[]{:S(2)}) async-start(), calls=%async_computation.3 | async-start | bytes 1572864 | tf_op jit(solution)/shard_map/all_gather | solution.py:17
  39.2 5.9 %copy-start.2 = (bf16[1024,256]{1,0:T(8,128)(2,1)S(1)}, bf16[1024,256]{1,0:T(8,128)(2,1)}, u32[]{:S(2)}) copy-start(bf16[1024,256]{1,0:T(8,128)(2,1)} %param.11) | copy-start | bytes 1572868
  39.2 6.9 %copy-start.3 = (bf16[1024,256]{1,0:T(8,128)(2,1)S(1)}, bf16[1024,256]{1,0:T(8,128)(2,1)}, u32[]{:S(2)}) copy-start(bf16[1024,256]{1,0:T(8,128)(2,1)} %param.12) | copy-start | bytes 1572868
  39.2 8.0 %copy-start.5 = (s32[1,16]{1,0:T(1,128)S(1)}, s32[1,16]{1,0:T(1,128)}, u32[]{:S(2)}) copy-start(s32[1,16]{1,0:T(1,128)} %param.19) | copy-start | bytes 196
  39.2 85.8 %all-to-all-start.1 = ((bf16[16,4,128,256]{3,2,1,0:T(8,128)(2,1)}), bf16[16,4,128,256]{3,2,1,0:T(8,128)(2,1)}, u32[]{:S(2)}, u32[]{:S(2)}) async-start(bf16[16,4,128,256]{3,2,1,0:T(8,128)(2,1)} %bitcast.38), calls=%async_computation.1 | async-start | bytes 8388608 | tf_op jit(solution)/shard_map/all_to_all | solution.py:27
  45.1 201.9 %all-reduce.3.cloned.1.call-start = ((), (), s32[]{:S(2)}) async-start(), calls=%async_computation.5 | async-start | bytes 1048576 | tf_op jit(solution)/shard_map/psum | solution.py:46
  47.2 201.6 %reduce-scatter.2.cloned.1.call-start = ((), (), s32[]{:S(2)}) async-start(), calls=%async_computation.4 | async-start | bytes 3145728 | tf_op jit(solution)/shard_map/reduce_scatter | solution.py:45
  132.0 116.8 %copy-start.4 = (bf16[256,256]{1,0:T(8,128)(2,1)S(1)}, bf16[256,256]{1,0:T(8,128)(2,1)}, u32[]{:S(2)}) copy-start(bf16[256,256]{1,0:T(8,128)(2,1)} %param.14) | copy-start | bytes 393220
  144.5 1.3 copy-start.1
Sparse Core Ops, SparseCore 0:
  11.2 23.9 all-gather.1
  146.0 46.1 reduce-scatter.1
Sparse Core Ops, SparseCore 1:
  51.6 195.3 all-reduce.2
where the time goes:
time: 259 us
  waiting for transfers between devices  183 us (71%)
  between operations  15.6 us (6%)
  other arithmetic  14.5 us (6%)
  blocking collectives  13.6 us (5%)
  matrix products  13.4 us (5%)
  local copies, waits for them, and re-layouts  12.8 us (5%)
  starting transfers between devices  5.93 us (2%)
    psum x1, waiting for transfers between devices, on_device(): self_sum, neigh_sum = lax.psum((terms_self, terms_neigh), ('blk', 'rep'))  101 us
    all_to_all x1, waiting for transfers between devices, on_device(): lax.all_to_all(found, 'blk', split_axis=0, concat_axis=0, tiled=True)  74.2 us
    all_to_all x1, blocking collectives, on_device(): lax.all_to_all(wanted, 'blk', split_axis=0, concat_axis=0, tiled=True)  13.6 us
    scatter-add x1, other arithmetic, on_device(): accumulated.at[target_rows].add(products.reshape(-1, side, width))  12.5 us
    all_gather x1, waiting for transfers between devices, on_device(): whole = lax.all_gather(share, 'rep', axis=0, tiled=True)  7.54 us
    dot_general x1, matrix products, on_device(): jnp.einsum('ikpq,ikqf->ikpf', chosen_tiles, fetched, preferred_element_ty...  6.73 us
    all_to_all x1, starting transfers between devices, on_device(): lax.all_to_all(found, 'blk', split_axis=0, concat_axis=0, tiled=True)  5.8 us
  transfers between devices with their start and end apart: 4, of which 3 were waited for; matrix products, arithmetic and copies ran while one was open for 12% of the time, Pallas kernels for 0%

commit v1 on v0

--- a/solution.py
+++ b/solution.py
@@ -1,7 +1,225 @@
+import functools
+
 import jax
 import jax.numpy as jnp
 from jax import lax
+from jax.experimental import pallas as pl
+from jax.experimental.pallas import tpu as pltpu
 from jax.sharding import PartitionSpec as P
+
+MESH = pl.DeviceIdType.MESH
+CORES, ROWS_Y = 2, 2
+
+
+def gather_kernel(blocks, own_ref, other_ref, g_ref, send_sem, recv_sem, x_sem, local_sem):
+    b = lax.axis_index("blk")
+    r = lax.axis_index("rep")
+    line = blocks // (CORES * ROWS_Y)
+    plane = CORES * ROWS_Y
+    z, y, c = b // plane, (b // CORES) % ROWS_Y, b % CORES
+    near_x = (b, 1 - r)
+    near_core = (z * plane + y * CORES + (1 - c), r)
+    near_y = (z * plane + (1 - y) * CORES + c, r)
+    up, down = (b + plane, r), (b - plane, r)
+    has_up, has_down = z < line - 1, z > 0
+
+    barrier = pltpu.get_barrier_semaphore()
+    for device in (near_x, near_core, near_y):
+        pl.semaphore_signal(barrier, inc=1, device_id=device, device_id_type=MESH)
+
+    @pl.when(has_up)
+    def _():
+        pl.semaphore_signal(barrier, inc=1, device_id=up, device_id_type=MESH)
+
+    @pl.when(has_down)
+    def _():
+        pl.semaphore_signal(barrier, inc=1, device_id=down, device_id_type=MESH)
+
+    expected = 3 + jnp.where(has_up, 1, 0) + jnp.where(has_down, 1, 0)
+    pl.semaphore_wait(barrier, expected)
+
+    def send(src, block, share, way, device):
+        return pltpu.make_async_remote_copy(
+            src_ref=src,
+            dst_ref=g_ref.at[block, share],
+            send_sem=send_sem.at[way, block, share],
+            recv_sem=recv_sem.at[block, share],
+            device_id=device,
+            device_id_type=MESH,
+        )
+
+    def arrived(block, share):
+        send(g_ref.at[block, share], block, share, 0, near_core).wait_recv()
+
+    x_copy = pltpu.make_async_remote_copy(
+        src_ref=other_ref,
+        dst_ref=g_ref.at[b, r],
+        send_sem=x_sem,
+        recv_sem=recv_sem.at[b, r],
+        device_id=near_x,
+        device_id_type=MESH,
+    )
+    x_copy.start()
+    keep = pltpu.make_async_copy(own_ref, g_ref.at[b, r], local_sem)
+    keep.start()
+
+    def spread_out(src, block, share, go_up, go_down):
+        @pl.when(go_up)
+        def _():
+            send(src, block, share, 0, up).start()
+
+        @pl.when(go_down)
+        def _():
+            send(src, block, share, 1, down).start()
+
+        send(src, block, share, 2, near_y).start()
+        send(src, block, share, 3, near_core).start()
+
+    shares = (r, 1 - r)
+    never = z < 0
+    spread_out(own_ref, b, r, has_up, has_down)
+    arrived(b, 1 - r)
+    spread_out(g_ref.at[b, 1 - r], b, 1 - r, has_up, has_down)
+
+    def from_y(distance, share):
+        for sign in (-1, 1) if distance else (0,):
+            other = z + sign * distance
+
+            @pl.when((other >= 0) & (other < line))
+            def _():
+                block = other * plane + (1 - y) * CORES + c
+                arrived(block, share)
+                send(g_ref.at[block, share], block, share, 3, near_core).start()
+
+    for distance in range(1, line):
+        for share in shares:
+
+            @pl.when(z - distance >= 0)
+            def _():
+                block = b - distance * plane
+                arrived(block, share)
+                spread_out(g_ref.at[block, share], block, share, has_up, never)
+
+            @pl.when(z + distance < line)
+            def _():
+                block = b + distance * plane
+                arrived(block, share)
+                spread_out(g_ref.at[block, share], block, share, never, has_down)
+
+        for share in shares:
+            from_y(distance - 1, share)
+    for share in shares:
+        from_y(line - 1, share)
+
+    keep.wait()
+    x_copy.wait_send()
+    for zz in range(line):
+        for share in shares:
+            for yy in (y, 1 - y):
+                mine = zz * plane + yy * CORES + c
+                arrived(zz * plane + yy * CORES + (1 - c), share)
+                send(own_ref, mine, share, 3, near_core).wait_send()
+            block = zz * plane + y * CORES + c
+            send(own_ref, block, share, 2, near_y).wait_send()
+
+            @pl.when((zz <= z) & has_up)
+            def _():
+                send(own_ref, block, share, 0, up).wait_send()
+
+            @pl.when((zz >= z) & has_down)
+            def _():
+                send(own_ref, block, share, 1, down).wait_send()
+
+
+def gather(own, other, blocks, copies):
+    rows, width = own.shape
+    return pl.pallas_call(
+        functools.partial(gather_kernel, blocks),
+        out_shape=jax.ShapeDtypeStruct((blocks, copies, rows, width), own.dtype),
+        in_specs=[pl.BlockSpec(memory_space=pltpu.VMEM)] * 2,
+        out_specs=pl.BlockSpec(memory_space=pl.ANY),
+        scratch_shapes=[
+            pltpu.SemaphoreType.DMA((4, blocks, copies)),
+            pltpu.SemaphoreType.DMA((blocks, copies)),
+            pltpu.SemaphoreType.DMA,
+            pltpu.SemaphoreType.DMA,
+        ],
+        compiler_params=pltpu.CompilerParams(collective_id=0, has_side_effects=True),
+        cost_estimate=pl.CostEstimate(
+            flops=0, bytes_accessed=blocks * copies * rows * width * 20, transcendentals=0
+        ),
+    )(own, other)
+
+
+def spread_kernel(rows, cols, counts, tiles_ref, g_ref, o_ref):
+    i = pl.program_id(0)
+    slots, side = tiles_ref.shape[1], tiles_ref.shape[2]
+
+    @pl.when(i == 0)
+    def _():
+        o_ref[...] = jnp.zeros_like(o_ref)
+
+    products = []
+    for k in range(slots):
+        start = pl.multiple_of(cols[i * slots + k] * side, side)
+        product = jnp.dot(
+            tiles_ref[0, k], g_ref[0, pl.ds(start, side), :], preferred_element_type=jnp.float32
+        )
+        products.append(jnp.where(k < counts[i], product, jnp.zeros_like(product)))
+    for k in range(slots):
+        o_ref[rows[i * slots + k]] += products[k]
+
+
+def spread_of(tiles, gathered, rows, cols, counts):
+    blocks, slots, side, _ = tiles.shape
+    depth, width = gathered.shape[1:]
+    return pl.pallas_call(
+        spread_kernel,
+        out_shape=jax.ShapeDtypeStruct((depth // side, side, width), jnp.float32),
+        grid_spec=pltpu.PrefetchScalarGridSpec(
+            num_scalar_prefetch=3,
+            grid=(blocks,),
+            in_specs=[
+                pl.BlockSpec((1, slots, side, side), lambda i, *_: (i, 0, 0, 0)),
+                pl.BlockSpec((1, depth, width), lambda i, *_: (i, 0, 0)),
+            ],
+            out_specs=pl.BlockSpec((depth // side, side, width), lambda i, *_: (0, 0, 0)),
+        ),
+    )(rows.reshape(-1), cols.reshape(-1), counts.reshape(-1), tiles, gathered)
+
+
+def by_columns(
+    features, aggregated, out_grad, w_self, w_neigh, tiles, tile_rows, tile_cols, tile_counts
+):
+    blocks, copies = lax.axis_size("blk"), lax.axis_size("rep")
+    r = lax.axis_index("rep")
+    rows, width = out_grad.shape
+    half = width // copies
+    side = tiles.shape[-1]
+    contract = (((0,), (0,)), ((), ()))
+    terms = tuple(
+        lax.dot_general(a, out_grad, contract, preferred_element_type=jnp.float32)
+        for a in (features, aggregated)
+    )
+    sums = lax.psum(terms, ("blk", "rep"))
+    weights = w_neigh.reshape(copies, half, width)
+
+    def message(which):
+        chosen = lax.dynamic_index_in_dim(weights, which, 0, keepdims=False)
+        return jnp.dot(out_grad, chosen.T, preferred_element_type=jnp.float32).astype(jnp.bfloat16)
+
+    gathered = gather(message(r), message(1 - r), blocks, copies)
+    gathered = gathered.reshape(blocks, copies * rows, half)
+    spread = spread_of(tiles[0], gathered, tile_rows[0], tile_cols[0], tile_counts[0])
+    spread = spread.reshape(copies, rows, half)
+    own = lax.dynamic_index_in_dim(spread, r, 0, keepdims=False)
+    sent = lax.dynamic_index_in_dim(spread, 1 - r, 0, keepdims=False).astype(jnp.bfloat16)
+    got = lax.ppermute(sent, "rep", [(0, 1), (1, 0)]).astype(jnp.float32)
+    left, right = jnp.where(r == 0, own, got), jnp.where(r == 0, got, own)
+    self_part = jnp.dot(out_grad, w_self.T, preferred_element_type=jnp.float32)
+    scale = (rows * blocks * copies) ** (-0.5)
+    feature_grad = self_part + jnp.concatenate([left, right], axis=1)
+    return (feature_grad, sums[0] * scale, sums[1] * scale)
 
 
 def on_device(
@@ -48,6 +266,8 @@
 
 
 def solution(mesh):
+    blocks, copies = mesh.shape["blk"], mesh.shape["rep"]
+    by_pairs = copies == 2 and blocks % (CORES * ROWS_Y) == 0
     placed = (
         P(("blk", "rep"), None),
         P(("blk", "rep"), None),
@@ -60,7 +280,7 @@
         P("blk", None),
     )
     return jax.shard_map(
-        on_device,
+        by_columns if by_pairs else on_device,
         mesh=mesh,
         in_specs=placed,
         out_specs=(P(("blk", "rep"), None), P(), P()),

time: 259 us -> 158 us (0.61)
  waiting for transfers between devices: 183 us -> 55.1 us
  Pallas kernels: 0 us -> 70.3 us
  blocking collectives: 13.6 us -> 0 us
  other arithmetic: 14.5 us -> 2.98 us
  local copies, waits for them, and re-layouts: 12.8 us -> 4.92 us
  starting transfers between devices: 5.93 us -> 0.67 us
  matrix products: 13.4 us -> 9.19 us
    all_to_all x1 -> x0, waiting for transfers between devices: 74.2 us -> none  [on_device(): lax.all_to_all(found, 'blk', split_axis=0, concat_axis=0, tiled=True)]
    pallas_call x0 -> x2, Pallas kernels: none -> 70.3 us  [the longest x1 56.8 us: gather(): pl.pallas_call(functools.partial(gather_kernel, blocks), out_shape=jax.Sh...]
    psum x1, waiting for transfers between devices: 101 us -> 55.1 us  [by_columns(): sums = lax.psum(terms, ('blk', 'rep'))]
    all_to_all x1 -> x0, blocking collectives: 13.6 us -> none  [on_device(): lax.all_to_all(wanted, 'blk', split_axis=0, concat_axis=0, tiled=True)]
    scatter-add x1 -> x0, other arithmetic: 12.5 us -> none  [on_device(): accumulated.at[target_rows].add(products.reshape(-1, side, width))]
    gather x4 -> x0, local copies, waits for them, and re-layouts: 9.62 us -> none  [the longest x1 3.98 us: on_device(): pieces_whole[lax.all_to_all(wanted, 'blk', split_axis=0, concat_axis=0, t...]
    all_gather x1 -> x0, waiting for transfers between devices: 7.54 us -> none  [on_device(): whole = lax.all_gather(share, 'rep', axis=0, tiled=True)]
    all_to_all x1 -> x0, starting transfers between devices: 5.8 us -> none  [on_device(): lax.all_to_all(found, 'blk', split_axis=0, concat_axis=0, tiled=True)]
  transfers between devices with their start and end apart: 4 -> 2, of which waited for: 3 -> 1; matrix products, arithmetic and copies ran while one was open for 12% -> 6% of each run, Pallas kernels for 0% -> 45%
where the time goes in v1:
time: 158 us; the launch traced here: 157 us
  Pallas kernels  70.3 us (44%)
  waiting for transfers between devices  55.1 us (35%)
  between operations  14.1 us (9%)
  matrix products  9.19 us (6%)
  local copies, waits for them, and re-layouts  4.92 us (3%)
  other arithmetic  2.98 us (2%)
    pallas_call x1, Pallas kernels, gather(): pl.pallas_call(functools.partial(gather_kernel, blocks), out_shape=jax.Sh...  56.8 us
    psum x1, waiting for transfers between devices, by_columns(): sums = lax.psum(terms, ('blk', 'rep'))  55.1 us
    pallas_call x1, Pallas kernels, spread_of(): pl.pallas_call(spread_kernel, out_shape=jax.ShapeDtypeStruct((depth // si...  13.5 us
    dot_general x2, matrix products, by_columns(): lax.dot_general(a, out_grad, contract, preferred_element_type=jnp.float32)  4.2 us
    dot_general x2, matrix products, message(): jnp.dot(out_grad, chosen.T, preferred_element_type=jnp.float32)  3.68 us
  transfers between devices with their start and end apart: 2, of which 1 were waited for; matrix products, arithmetic and copies ran while one was open for 6% of the time, Pallas kernels for 45%

profile of v1, /device:TPU:0, one launch (start us, length us, event | category | flops | bytes accessed | tf_op | source)
XLA Modules:
  0.0 157.3 jit_solution(6052463371129805380)
XLA Ops:
  7.2 0.0 copy-start
  7.2 0.0 all-reduce.3.cloned.1.call-start
  7.2 1.0 copy-done
  8.2 2.1 %fusion.10 = f32[256,256]{1,0:T(8,128)} fusion(bf16[1024,256]{1,0:T(8,128)(2,1)} %param.10, bf16[1024,256]{1,0:T(8,128)(2,1)S(1)} %copy-done), kind=kOutput, calls=%fused_computation.18 | convolution fusion | flops 134217728 | bytes 1310720 | tf_op jit(solution)/shard_map/dot_general | solution.py:201
  10.3 2.1 %fusion.9 = f32[256,256]{1,0:T(8,128)} fusion(bf16[1024,256]{1,0:T(8,128)(2,1)} %param.9, bf16[1024,256]{1,0:T(8,128)(2,1)S(1)} %copy-done), kind=kOutput, calls=%fused_computation.17 | convolution fusion | flops 134217728 | bytes 1310720 | tf_op jit(solution)/shard_map/dot_general | solution.py:201
  12.4 0.0 all-reduce.3.cloned.1.call-update
  12.4 0.8 copy.16
  13.2 0.7 reshape_squeeze.6.rows
  13.9 0.8 copy.17
  14.6 0.7 reshape_squeeze.7.cols
  15.3 1.8 %fusion.1.other_ref = bf16[1024,128]{1,0:T(8,128)(2,1)} fusion(bf16[1024,256]{1,0:T(8,128)(2,1)S(1)} %copy-done, bf16[2,128,256]{2,1,0:T(8,128)(2,1)} %bitcast.32, s32[]{:T(128)S(6)} %select_n.24), kind=kOutput, calls=%fused_computation.3 | convolution fusion | flops 67239936 | bytes 851972 | tf_op jit(solution)/shard_map/dot_general | solution.py:209
  17.1 1.8 %fusion.own_ref = bf16[1024,128]{1,0:T(8,128)(2,1)} fusion(bf16[1024,256]{1,0:T(8,128)(2,1)S(1)} %copy-done, bf16[2,128,256]{2,1,0:T(8,128)(2,1)} %bitcast.33, s32[]{:T(128)S(6)} %select_n.23), kind=kOutput, calls=%fused_computation.2 | convolution fusion | flops 67239936 | bytes 851972 | tf_op jit(solution)/shard_map/dot_general | solution.py:209
  19.0 56.8 %shard_map.112 = bf16[16,2,1024,128]{3,2,1,0:T(8,128)(2,1)} custom-call(bf16[1024,128]{1,0:T(8,128)(2,1)} %fusion.own_ref, bf16[1024,128]{1,0:T(8,128)(2,1)} %fusion.1.other_ref), custom_call_target="tpu_custom_call" | custom-call | bytes 83886080 | tf_op jit(solution)/shard_map/pallas_call | solution.py:136
  75.8 0.0 copy-start.1
  75.8 13.5 %shard_map.113 = f32[16,128,128]{2,1,0:T(8,128)} custom-call(s32[128]{0:T(128)} %reshape_squeeze.6.rows, s32[128]{0:T(128)} %reshape_squeeze.7.cols, s32[16]{0:T(128)} %bitcast.34, bf16[16,8,128,128]{3,2,1,0:T(8,128)(2,1)} %bitcast.29, bf16[16,2048,128]{2,1,0:T(8,128)(2,1)} %bitcast.28), custom_call_target="tpu_custom_call" | custom-call | tf_op jit(solution)/shard_map/pallas_call | solution.py:176
  89.3 1.1 fusion.2
  90.4 0.6 collective-permute-start
  91.0 55.1 %all-reduce.3.cloned.1.call-done = (f32[256,256]{1,0:T(8,128)}, f32[256,256]{1,0:T(8,128)}) async-done(((f32[256,256]{1,0:T(8,128)}, f32[256,256]{1,0:T(8,128)}), (f32[256,256]{1,0:T(8,128)}, f32[256,256]{1,0:T(8,128)})) %all-reduce.3.cloned.1.call-update) | async-done | bytes 524304 | tf_op jit(solution)/shard_map/psum | solution.py:204
  146.1 1.9 %broadcast_multiply_fusion = (f32[256,256]{1,0:T(8,128)}, f32[256,256]{1,0:T(8,128)}) fusion(f32[256,256]{1,0:T(8,128)} %get-tuple-element.4, f32[256,256]{1,0:T(8,128)} %get-tuple-element.3), kind=kLoop, calls=%fused_computation.9 | loop fusion | flops 131072 | bytes 1048576 | tf_op jit(solution)/shard_map/mul | solution.py:222
  148.0 0.0 collective-permute-done
  148.0 1.1 convert_select_fusion.1
  149.1 0.0 copy-done.1
  149.1 1.3 maximum_add_fusion
Async XLA Ops:
  7.2 1.0 copy-start
  7.2 138.9 %all-reduce.3.cloned.1.call-start = ((), (), s32[]{:S(2)}) async-start(), calls=%async_computation | async-start | bytes 1048576 | tf_op jit(solution)/shard_map/psum | solution.py:204
  75.8 73.3 %copy-start.1 = (bf16[256,256]{1,0:T(8,128)(2,1)S(1)}, bf16[256,256]{1,0:T(8,128)(2,1)}, u32[]{:S(2)}) copy-start(bf16[256,256]{1,0:T(8,128)(2,1)} %param.12) | copy-start | bytes 393220
  90.4 57.6 %collective-permute-start = (bf16[1024,128]{1,0:T(8,128)(2,1)S(1)}, bf16[1024,128]{1,0:T(8,128)(2,1)S(1)}, u32[]{:S(2)}, u32[]{:S(2)}) collective-permute-start(bf16[1024,128]{1,0:T(8,128)(2,1)S(1)} %fusion.2), channel_id=1, source_target_pairs={{0,1},{1,0},{2,3},{3,2},{4,5},{5,4},{6,7},{7,6},{8,9},{9,8},{10,11... | collective-permute-start | bytes 786440 | tf_op jit(solution)/shard_map/ppermute | solution.py:217
Sparse Core Ops, SparseCore 0:
  13.4 132.6 all-reduce.2

commit v2 on v1

--- a/solution.py
+++ b/solution.py
@@ -11,7 +11,26 @@
 CORES, ROWS_Y = 2, 2
 
 
-def gather_kernel(blocks, own_ref, other_ref, g_ref, send_sem, recv_sem, x_sem, local_sem):
+def gather_kernel(
+    blocks,
+    copies,
+    scale,
+    own_ref,
+    other_ref,
+    terms_ref,
+    g_ref,
+    sum_ref,
+    parts,
+    total,
+    send_sem,
+    recv_sem,
+    x_sem,
+    local_sem,
+    part_send,
+    part_recv,
+    total_send,
+    total_recv,
+):
     b = lax.axis_index("blk")
     r = lax.axis_index("rep")
     line = blocks // (CORES * ROWS_Y)
@@ -24,19 +43,64 @@
     has_up, has_down = z < line - 1, z > 0
 
     barrier = pltpu.get_barrier_semaphore()
-    for device in (near_x, near_core, near_y):
-        pl.semaphore_signal(barrier, inc=1, device_id=device, device_id_type=MESH)
-
-    @pl.when(has_up)
-    def _():
-        pl.semaphore_signal(barrier, inc=1, device_id=up, device_id_type=MESH)
-
-    @pl.when(has_down)
-    def _():
-        pl.semaphore_signal(barrier, inc=1, device_id=down, device_id_type=MESH)
-
-    expected = 3 + jnp.where(has_up, 1, 0) + jnp.where(has_down, 1, 0)
-    pl.semaphore_wait(barrier, expected)
+    devices = blocks * copies
+    me = b * copies + r
+
+    def peer_of(step):
+        peer = (me + step) % devices
+        return peer, (peer // copies, peer % copies)
+
+    @pl.loop(1, devices)
+    def _(step):
+        pl.semaphore_signal(barrier, inc=1, device_id=peer_of(step)[1], device_id_type=MESH)
+
+    pl.semaphore_wait(barrier, devices - 1)
+
+    def part_copy(step):
+        peer, device = peer_of(step)
+        return pltpu.make_async_remote_copy(
+            src_ref=terms_ref.at[peer],
+            dst_ref=parts.at[me],
+            send_sem=part_send.at[peer],
+            recv_sem=part_recv.at[me],
+            device_id=device,
+            device_id_type=MESH,
+        )
+
+    def part_from(step):
+        peer, device = peer_of(step)
+        return pltpu.make_async_remote_copy(
+            src_ref=terms_ref.at[peer],
+            dst_ref=parts.at[peer],
+            send_sem=part_send.at[peer],
+            recv_sem=part_recv.at[peer],
+            device_id=device,
+            device_id_type=MESH,
+        )
+
+    def total_copy(step, slot):
+        peer, device = peer_of(step)
+        return pltpu.make_async_remote_copy(
+            src_ref=total.at[me],
+            dst_ref=total.at[slot],
+            send_sem=total_send.at[peer],
+            recv_sem=total_recv.at[slot],
+            device_id=device,
+            device_id_type=MESH,
+        )
+
+    def add_parts():
+        parts[me] = terms_ref[me]
+
+        @pl.loop(1, devices)
+        def _(step):
+            part_from(step).wait_recv()
+
+        total[me] = jnp.sum(parts[...], axis=0) * scale
+
+        @pl.loop(1, devices)
+        def _(step):
+            total_copy(step, me).start()
 
     def send(src, block, share, way, device):
         return pltpu.make_async_remote_copy(
@@ -78,6 +142,11 @@
     shares = (r, 1 - r)
     never = z < 0
     spread_out(own_ref, b, r, has_up, has_down)
+
+    @pl.loop(1, devices)
+    def _(step):
+        part_copy(step).start()
+
     arrived(b, 1 - r)
     spread_out(g_ref.at[b, 1 - r], b, 1 - r, has_up, has_down)
 
@@ -108,9 +177,18 @@
 
         for share in shares:
             from_y(distance - 1, share)
+        if distance == 1:
+            add_parts()
     for share in shares:
         from_y(line - 1, share)
 
+    @pl.loop(1, devices)
+    def _(step):
+        part_copy(step).wait_send()
+        total_copy(step, me).wait_send()
+        total_copy(step, peer_of(step)[0]).wait_recv()
+
+    sum_ref[...] = total[...]
     keep.wait()
     x_copy.wait_send()
     for zz in range(line):
@@ -131,24 +209,37 @@
                 send(own_ref, block, share, 1, down).wait_send()
 
 
-def gather(own, other, blocks, copies):
+def gather(own, other, terms, scale, blocks, copies):
+    devices = blocks * copies
     rows, width = own.shape
     return pl.pallas_call(
-        functools.partial(gather_kernel, blocks),
-        out_shape=jax.ShapeDtypeStruct((blocks, copies, rows, width), own.dtype),
-        in_specs=[pl.BlockSpec(memory_space=pltpu.VMEM)] * 2,
-        out_specs=pl.BlockSpec(memory_space=pl.ANY),
+        functools.partial(gather_kernel, blocks, copies, scale),
+        out_shape=(
+            jax.ShapeDtypeStruct((blocks, copies, rows, width), own.dtype),
+            jax.ShapeDtypeStruct(terms.shape, terms.dtype),
+        ),
+        in_specs=[pl.BlockSpec(memory_space=pltpu.VMEM)] * 3,
+        out_specs=(
+            pl.BlockSpec(memory_space=pl.ANY),
+            pl.BlockSpec(memory_space=pltpu.VMEM),
+        ),
         scratch_shapes=[
+            pltpu.VMEM(terms.shape, terms.dtype),
+            pltpu.VMEM(terms.shape, terms.dtype),
             pltpu.SemaphoreType.DMA((4, blocks, copies)),
             pltpu.SemaphoreType.DMA((blocks, copies)),
             pltpu.SemaphoreType.DMA,
             pltpu.SemaphoreType.DMA,
+            pltpu.SemaphoreType.DMA((devices,)),
+            pltpu.SemaphoreType.DMA((devices,)),
+            pltpu.SemaphoreType.DMA((devices,)),
+            pltpu.SemaphoreType.DMA((devices,)),
         ],
         compiler_params=pltpu.CompilerParams(collective_id=0, has_side_effects=True),
         cost_estimate=pl.CostEstimate(
             flops=0, bytes_accessed=blocks * copies * rows * width * 20, transcendentals=0
         ),
-    )(own, other)
+    )(own, other, terms)
 
 
 def spread_kernel(rows, cols, counts, tiles_ref, g_ref, o_ref):
@@ -197,18 +288,23 @@
     half = width // copies
     side = tiles.shape[-1]
     contract = (((0,), (0,)), ((), ()))
-    terms = tuple(
-        lax.dot_general(a, out_grad, contract, preferred_element_type=jnp.float32)
-        for a in (features, aggregated)
-    )
-    sums = lax.psum(terms, ("blk", "rep"))
+    devices = blocks * copies
+    terms = jnp.concatenate(
+        [
+            lax.dot_general(a, out_grad, contract, preferred_element_type=jnp.float32)
+            for a in (features, aggregated)
+        ]
+    )
+    terms = terms.reshape(devices, -1, width)
+    scale = (rows * devices) ** (-0.5)
     weights = w_neigh.reshape(copies, half, width)
 
     def message(which):
         chosen = lax.dynamic_index_in_dim(weights, which, 0, keepdims=False)
         return jnp.dot(out_grad, chosen.T, preferred_element_type=jnp.float32).astype(jnp.bfloat16)
 
-    gathered = gather(message(r), message(1 - r), blocks, copies)
+    gathered, sums = gather(message(r), message(1 - r), terms, scale, blocks, copies)
+    sums = sums.reshape(2, width, width)
     gathered = gathered.reshape(blocks, copies * rows, half)
     spread = spread_of(tiles[0], gathered, tile_rows[0], tile_cols[0], tile_counts[0])
     spread = spread.reshape(copies, rows, half)
@@ -217,9 +313,8 @@
     got = lax.ppermute(sent, "rep", [(0, 1), (1, 0)]).astype(jnp.float32)
     left, right = jnp.where(r == 0, own, got), jnp.where(r == 0, got, own)
     self_part = jnp.dot(out_grad, w_self.T, preferred_element_type=jnp.float32)
-    scale = (rows * blocks * copies) ** (-0.5)
     feature_grad = self_part + jnp.concatenate([left, right], axis=1)
-    return (feature_grad, sums[0] * scale, sums[1] * scale)
+    return (feature_grad, sums[0], sums[1])
 
 
 def on_device(

time: 158 us -> 109 us (0.69)
  waiting for transfers between devices: 55.1 us -> 7.17 us
  Pallas kernels: 70.3 us -> 85.2 us
  between operations: 14.1 us -> 0.7 us
    psum x1 -> x0, waiting for transfers between devices: 55.1 us -> none  [by_columns(): sums = lax.psum(terms, ('blk', 'rep'))]
    pallas_call x1, Pallas kernels: 56.8 us -> 71.8 us  [gather(): pl.pallas_call(functools.partial(gather_kernel, blocks, copies, scale), o...]
    ppermute x1, waiting for transfers between devices: 0.01 us -> 7.17 us  [by_columns(): got = lax.ppermute(sent, 'rep', [(0, 1), (1, 0)]).astype(jnp.float32)]
    mul x1 -> x0, other arithmetic: 1.86 us -> none  [by_columns(): return (feature_grad, sums[0] * scale, sums[1] * scale)]
  transfers between devices with their start and end apart: 2 -> 1, of which waited for: 1 -> 1; matrix products, arithmetic and copies ran while one was open for 6% -> 1% of each run, Pallas kernels for 45% -> 0%
where the time goes in v2:
time: 109 us; the launch traced here: 108 us
  Pallas kernels  85.2 us (78%)
  matrix products  7.73 us (7%)
  waiting for transfers between devices  7.17 us (7%)
  local copies, waits for them, and re-layouts  4.78 us (4%)
  other arithmetic  1.94 us (2%)
    pallas_call x1, Pallas kernels, gather(): pl.pallas_call(functools.partial(gather_kernel, blocks, copies, scale), o...  71.8 us
    pallas_call x1, Pallas kernels, spread_of(): pl.pallas_call(spread_kernel, out_shape=jax.ShapeDtypeStruct((depth // si...  13.4 us
    ppermute x1, waiting for transfers between devices, by_columns(): got = lax.ppermute(sent, 'rep', [(0, 1), (1, 0)]).astype(jnp.float32)  7.17 us
    dot_general x2, matrix products, message(): jnp.dot(out_grad, chosen.T, preferred_element_type=jnp.float32)  3.68 us
    dot_general x2, matrix products, by_columns(): lax.dot_general(a, out_grad, contract, preferred_element_type=jnp.float32)  2.75 us
  transfers between devices with their start and end apart: 1, of which 1 were waited for; matrix products, arithmetic and copies ran while one was open for 1% of the time, Pallas kernels for 0%

profile of v2, /device:TPU:0, one launch (start us, length us, event | category | flops | bytes accessed | tf_op | source)
XLA Modules:
  0.0 108.2 jit_solution(7123292062404437673)
XLA Ops:
  0.6 0.0 copy-start
  0.6 0.8 copy.16
  1.5 0.6 reshape_squeeze.6.rows
  2.1 0.8 copy.17
  2.8 0.7 reshape_squeeze.7.cols
  3.5 0.0 copy-done
  3.5 1.4 %fusion.10 = f32[256,256]{1,0:T(8,128)S(1)} fusion(bf16[1024,256]{1,0:T(8,128)(2,1)} %param.9, bf16[1024,256]{1,0:T(8,128)(2,1)S(1)} %copy-done), kind=kOutput, calls=%fused_computation.17 | convolution fusion | flops 134217728 | bytes 1310720 | tf_op jit(solution)/shard_map/dot_general | solution.py:294
  4.9 1.4 %fusion.11 = f32[256,256]{1,0:T(8,128)S(1)} fusion(bf16[1024,256]{1,0:T(8,128)(2,1)} %param.10, bf16[1024,256]{1,0:T(8,128)(2,1)S(1)} %copy-done), kind=kOutput, calls=%fused_computation.18 | convolution fusion | flops 134217728 | bytes 1310720 | tf_op jit(solution)/shard_map/dot_general | solution.py:294
  6.3 1.8 %fusion.1.other_ref = bf16[1024,128]{1,0:T(8,128)(2,1)} fusion(bf16[1024,256]{1,0:T(8,128)(2,1)S(1)} %copy-done, bf16[2,128,256]{2,1,0:T(8,128)(2,1)} %bitcast.38, s32[]{:T(128)S(6)} %select_n.24), kind=kOutput, calls=%fused_computation.3 | convolution fusion | flops 67239936 | bytes 851972 | tf_op jit(solution)/shard_map/dot_general | solution.py:304
  8.1 1.8 %fusion.own_ref = bf16[1024,128]{1,0:T(8,128)(2,1)} fusion(bf16[1024,256]{1,0:T(8,128)(2,1)S(1)} %copy-done, bf16[2,128,256]{2,1,0:T(8,128)(2,1)} %bitcast.39, s32[]{:T(128)S(6)} %select_n.23), kind=kOutput, calls=%fused_computation.2 | convolution fusion | flops 67239936 | bytes 851972 | tf_op jit(solution)/shard_map/dot_general | solution.py:304
  10.0 0.8 pad_maximum_fusion
  10.8 71.8 %shard_map.112 = (bf16[16,2,1024,128]{3,2,1,0:T(8,128)(2,1)}, f32[32,16,256]{2,1,0:T(8,128)}) custom-call(bf16[1024,128]{1,0:T(8,128)(2,1)} %fusion.own_ref, bf16[1024,128]{1,0:T(8,128)(2,1)} %fusion.1.other_ref, f32[32,16,256]{2,1,0:T(8,128)} %bitcast.35), custom_call_target="tpu_custom_call" | custom-call | bytes 83886080 | tf_op jit(solution)/shard_map/pallas_call | solution.py:215
  82.6 0.0 copy-start.1
  82.6 0.0 copy-start.2
  82.6 13.4 %shard_map.113 = f32[16,128,128]{2,1,0:T(8,128)} custom-call(s32[128]{0:T(128)} %reshape_squeeze.6.rows, s32[128]{0:T(128)} %reshape_squeeze.7.cols, s32[16]{0:T(128)} %bitcast.40, bf16[16,8,128,128]{3,2,1,0:T(8,128)(2,1)} %bitcast.32, bf16[16,2048,128]{2,1,0:T(8,128)(2,1)} %bitcast.31), custom_call_target="tpu_custom_call" | custom-call | tf_op jit(solution)/shard_map/pallas_call | solution.py:267
  96.1 1.1 fusion.2
  97.1 0.7 collective-permute-start
  97.8 0.0 copy-done.1
  97.8 0.8 fusion.9
  98.6 7.2 %collective-permute-done = bf16[1024,128]{1,0:T(8,128)(2,1)S(1)} collective-permute-done((bf16[1024,128]{1,0:T(8,128)(2,1)S(1)}, bf16[1024,128]{1,0:T(8,128)(2,1)S(1)}, u32[]{:S(2)}, u32[]{:S(2)}) %collective-permute-start) | collective-permute-done | bytes 262176 | tf_op jit(solution)/shard_map/ppermute | solution.py:313
  105.8 1.1 %convert_select_fusion.1 = (f32[1024,128]{1,0:T(8,128)S(1)}, f32[1024,128]{1,0:T(8,128)S(1)}) fusion(bf16[1024,128]{1,0:T(8,128)(2,1)S(1)} %collective-permute-done, f32[2,1024,128]{2,1,0:T(8,128)} %bitcast.34, s32[]{:T(128)S(6)} %select_n.23, pred[]{:T(512)S(6)} %eq.4), kind=kLoop, calls=%fused_computation.6 | loop fusion | flops 393216 | bytes 1835013 | tf_op jit(solution)/shard_map/jit(_where)/select_n | solution.py:314
  106.9 0.0 copy-done.2
  106.9 1.3 %maximum_add_fusion = f32[1024,256]{1,0:T(8,128)} fusion(f32[1024,128]{1,0:T(8,128)S(1)} %get-tuple-element.8, f32[1024,128]{1,0:T(8,128)S(1)} %get-tuple-element.7, bf16[1024,256]{1,0:T(8,128)(2,1)S(1)} %copy-done, bf16[256,256]{1,0:T(8,128)(2,1)S(1)} %copy-done.2), kind=kOutput, calls=%fused_computation.4 | convolution fusion | flops 134742016 | bytes 2752512 | tf_op jit(solution)/shard_map/dot_general | solution.py:315
Async XLA Ops:
  0.6 2.9 %copy-start = (bf16[1024,256]{1,0:T(8,128)(2,1)S(1)}, bf16[1024,256]{1,0:T(8,128)(2,1)}, u32[]{:S(2)}) copy-start(bf16[1024,256]{1,0:T(8,128)(2,1)} %param.11) | copy-start | bytes 1572868
  82.6 15.2 %copy-start.1 = (f32[32,16,256]{2,1,0:T(8,128)S(1)}, f32[32,16,256]{2,1,0:T(8,128)}, u32[]{:S(2)}) copy-start(f32[32,16,256]{2,1,0:T(8,128)} %get-tuple-element.6) | copy-start | bytes 1572868
  82.6 24.3 %copy-start.2 = (bf16[256,256]{1,0:T(8,128)(2,1)S(1)}, bf16[256,256]{1,0:T(8,128)(2,1)}, u32[]{:S(2)}) copy-start(bf16[256,256]{1,0:T(8,128)(2,1)} %param.12) | copy-start | bytes 393220
  97.1 8.7 %collective-permute-start = (bf16[1024,128]{1,0:T(8,128)(2,1)S(1)}, bf16[1024,128]{1,0:T(8,128)(2,1)S(1)}, u32[]{:S(2)}, u32[]{:S(2)}) collective-permute-start(bf16[1024,128]{1,0:T(8,128)(2,1)S(1)} %fusion.2), channel_id=1, source_target_pairs={{0,1},{1,0},{2,3},{3,2},{4,5},{5,4},{6,7},{7,6},{8,9},{9,8},{10,11... | collective-permute-start | bytes 786440 | tf_op jit(solution)/shard_map/ppermute | solution.py:313
